TPU v7x, 512 devices: a whole 4x8x8 slice. The times are simulated.
512 devices in a mesh: dp: 16 (over x_hi, y), ctx: 32 (over z, x_lo, core).
Axes of the slice: x: 4 (x_hi: 2, x_lo: 2; x = x_hi * 2 + x_lo), y: 8, z: 8, core: 2. Of those that a mesh axis runs over, the one named last changes fastest.
Arguments:
- tokens: bfloat16 [16, 4096, 8192], P('dp', 'ctx')
- qkv_weight: bfloat16 [8192, 384], P('dp')
- out_grad: bfloat16 [16, 4096, 128], P('dp', 'ctx'), may hold values from -0.0625 to 0.0625
Outputs:
- attn_out: bfloat16 [16, 4096, 128], P('dp', 'ctx')
- qkv_grad: bfloat16 [8192, 384], P('dp')
All inputs are finite; a program needn't handle non-finite values.
Results may differ from a plain program's by a relative error of at most 0.03.
Values may be sent and summed in bfloat16 or wider, within the bound.
No kernel may reach another device: no remote copies, remote signals or barrier semaphores. Data moves between devices by JAX's collectives and lax.ppermute only.
A program may use at most 64 MiB of HBM per device.

v0:
```python
import math
import jax
import jax.numpy as jnp
from jax import lax
from jax.sharding import PartitionSpec as P

z_weight = 0.001
masked_fill = -1e30


def stored_positions(first_row, number, half_rows, ctx_count):
    indices = first_row + jnp.arange(number, dtype=jnp.int32)
    device_index = indices // (2 * half_rows)
    inside = indices % (2 * half_rows)
    block_index = jnp.where(inside < half_rows, device_index, 2 * ctx_count - 1 - device_index)
    return block_index * half_rows + inside % half_rows


def contract_last(left, right):
    return lax.dot_general(
        left, right, (((1,), (1,)), ((), ())), preferred_element_type=jnp.float32
    )


def contract_first(left, right):
    return lax.dot_general(
        left, right, (((0,), (0,)), ((), ())), preferred_element_type=jnp.float32
    )


def on_device(tokens, qkv_weight, out_grad):
    ctx_count = lax.axis_size("ctx")
    feature_rows = tokens[0]
    cotangent = out_grad[0]
    row_count = feature_rows.shape[0]
    half_rows = row_count // 2
    width = qkv_weight.shape[1]
    head_size = width // 3
    score_scale = 1.0 / math.sqrt(head_size)
    columns = lax.all_to_all(tokens, "dp", split_axis=2, concat_axis=0, tiled=True)
    flat_columns = columns.reshape(-1, columns.shape[2])
    projected = jnp.dot(
        feature_rows,
        lax.all_gather(qkv_weight, "dp", axis=0, tiled=True),
        preferred_element_type=jnp.float32,
    )
    qkv = projected.astype(jnp.bfloat16)
    queries = qkv[:, :head_size]
    own_pairs = qkv[:, head_size:]
    gathered = lax.all_gather(own_pairs, "ctx", axis=0, tiled=True)
    key_rows = gathered[:, :head_size]
    value_rows = gathered[:, head_size:]
    own_positions = stored_positions(
        lax.axis_index("ctx") * row_count, row_count, half_rows, ctx_count
    )
    all_positions = stored_positions(0, row_count * ctx_count, half_rows, ctx_count)
    allowed = all_positions[None, :] <= own_positions[:, None]
    scores = jnp.where(allowed, contract_last(queries, key_rows) * score_scale, masked_fill)
    row_top = jnp.max(scores, axis=1)
    log_total = row_top + jnp.log(jnp.sum(jnp.exp(scores - row_top[:, None]), axis=1))
    probs = jnp.where(allowed, jnp.exp(scores - log_total[:, None]), 0.0)
    probs_low = probs.astype(jnp.bfloat16)
    attn_rows = jnp.dot(probs_low, value_rows, preferred_element_type=jnp.float32).astype(
        jnp.bfloat16
    )
    row_delta = jnp.sum(cotangent.astype(jnp.float32) * attn_rows.astype(jnp.float32), axis=1)
    dprob = contract_last(cotangent, value_rows)
    dscore = probs * (dprob - row_delta[:, None] + 2.0 * z_weight * log_total[:, None])
    dscore_low = dscore.astype(jnp.bfloat16)
    grad_query = (
        jnp.dot(dscore_low, key_rows, preferred_element_type=jnp.float32) * score_scale
    ).astype(jnp.bfloat16)
    query_all, cotangent_all = (
        lax.all_gather(queries, "ctx", axis=0, tiled=True),
        lax.all_gather(cotangent, "ctx", axis=0, tiled=True),
    )
    total_all, delta_all = (
        lax.all_gather(log_total, "ctx", axis=0, tiled=True),
        lax.all_gather(row_delta, "ctx", axis=0, tiled=True),
    )
    own_keys = own_pairs[:, :head_size]
    own_values = own_pairs[:, head_size:]
    allowed_back = own_positions[None, :] <= all_positions[:, None]
    scores_back = jnp.where(
        allowed_back, contract_last(query_all, own_keys) * score_scale, masked_fill
    )
    probs_back = jnp.where(allowed_back, jnp.exp(scores_back - total_all[:, None]), 0.0)
    dprob_back = contract_last(cotangent_all, own_values)
    dscore_back = probs_back * (
        dprob_back - delta_all[:, None] + 2.0 * z_weight * total_all[:, None]
    )
    grad_key = (contract_first(dscore_back.astype(jnp.bfloat16), query_all) * score_scale).astype(
        jnp.bfloat16
    )
    grad_value = contract_first(probs_back.astype(jnp.bfloat16), cotangent_all).astype(jnp.bfloat16)
    grad_rows = jnp.concatenate([grad_query, grad_key, grad_value], axis=1)
    partial_sum = contract_first(flat_columns, lax.all_gather(grad_rows, "dp", axis=0, tiled=True))
    weight_total = lax.psum(partial_sum.astype(jnp.bfloat16), "ctx")
    return (attn_rows[None], weight_total)


def solution(mesh):
    placed = (P("dp", "ctx", None), P("dp", None), P("dp", "ctx", None))
    return jax.shard_map(
        on_device,
        mesh=mesh,
        in_specs=placed,
        out_specs=(P("dp", "ctx", None), P("dp", None)),
        check_vma=False,
    )
```

profile of v0, /device:TPU:4, one launch (start us, length us, event | category | flops | bytes accessed | tf_op | source)
XLA Modules:
  0.0 672.1 jit_solution(11417274959753456730)
XLA Ops:
  7.2 0.0 all-gather.9.cloned.1.call-start
  7.2 0.7 all-gather.9.cloned.1.call-update
  7.9 0.0 copy-start
  7.9 0.0 all-gather.11.cloned.1.call-start
  8.0 126.6 %all-gather.9.cloned.1.call-done = bf16[8192,384]{1,0:T(8,128)(2,1)} async-done(((bf16[512,384]{1,0:T(8,128)(2,1)}), bf16[8192,384]{1,0:T(8,128)(2,1)}) %all-gather.9.cloned.1.call-update) | async-done | bytes 6291472 | tf_op jit(solution)/shard_map/all_gather | solution.py:44
  134.5 4.7 fusion.19
  139.2 0.6 slice.27
  139.8 0.0 all-gather.11.cloned.1.call-update
  139.9 0.0 all-gather.13.cloned.1.call-start
  139.9 0.6 slice.26
  140.5 0.1 all-gather.13.cloned.1.call-update
  140.6 0.0 all-gather.17.cloned.1.call-start
  140.6 0.5 all-gather.17.cloned.1.call-update
  141.2 0.0 copy-done
  141.2 6.8 %copy.21 = bf16[1,128,8192]{1,0,2:T(2,128)(2,1)} copy(bf16[1,128,8192]{2,1,0:T(8,128)(2,1)S(1)} %copy-done) | data formatting | bytes 4194304 | tf_op args[0]
  148.0 0.6 broadcast.369
  148.6 45.2 %reduce = bf16[8192,128]{1,0:T(8,128)(2,1)S(1)} reduce(bf16[8192,1,128]{2,1,0:T(2,128)(2,1)} %bitcast.59, bf16[]{:T(256)} %broadcast.369), dimensions={1}, to_apply=%bitcast.52.reduce_sub_computation | reduce | bytes 4194306
  193.8 2.1 reshape.196
  195.9 0.0 copy-start.3
  195.9 7.6 %all-to-all-start = ((bf16[16,2,32768]{2,1,0:T(2,128)(2,1)}), bf16[16,2,32768]{2,1,0:T(2,128)(2,1)S(1)}, u32[]{:S(2)}, u32[]{:S(2)}) async-start(bf16[16,2,32768]{2,1,0:T(2,128)(2,1)} %reshape.196), calls=%async_computation | async-start | bytes 4194304 | tf_op jit(solution)/shard_map/all_to_all | solution.py:40
  203.5 0.0 all-gather.15.cloned.1.call-start
  203.5 0.0 copy-done.3
  203.5 0.1 copy.18
  203.7 3.5 all-gather.11.cloned.1.call-done
  207.2 0.0 copy-start.4
  207.2 1.9 fusion.69
  209.1 0.0 copy-start.2
  209.1 0.4 exponential_reduce_fusion
  209.6 0.0 copy-done.4
  209.6 0.7 multiply_reduce_fusion
  210.3 0.1 copy-done.2
  210.4 32.5 %all-gather.2 = f32[32,1,128]{2,1,0:T(1,128)S(1)} all-gather(f32[1,1,128]{2,1,0:T(1,128)S(1)} %bitcast.68), channel_id=1, replica_groups=mesh['dp'=16,'ctx'=32] {'ctx'}, dimensions={0}, use_global_device_ids=true | all-gather | bytes 16896 | tf_op jit(solution)/shard_map/all_gather | solution.py:79
  242.9 30.6 %all-gather.1 = f32[32,1,128]{2,1,0:T(1,128)S(1)} all-gather(f32[1,1,128]{2,1,0:T(1,128)S(1)} %bitcast.67), channel_id=1, replica_groups=mesh['dp'=16,'ctx'=32] {'ctx'}, dimensions={0}, use_global_device_ids=true | all-gather | bytes 16896 | tf_op jit(solution)/shard_map/all_gather | solution.py:78
  273.5 2.5 all-gather.13.cloned.1.call-done
  276.1 3.3 fusion.6
  279.4 68.4 %all-gather.17.cloned.1.call-done = bf16[1,4096,128]{2,1,0:T(8,128)(2,1)} async-done(((bf16[1,128,128]{2,1,0:T(8,128)(2,1)}), bf16[1,4096,128]{2,1,0:T(8,128)(2,1)}) %all-gather.17.cloned.1.call-update) | async-done | bytes 1048592 | tf_op jit(solution)/shard_map/all_gather | solution.py:75
  347.8 0.0 copy-start.1
  347.8 2.4 convolution_convert_fusion.1
  350.3 0.0 copy-done.1
  350.3 3.5 fusion.24
  353.8 3.2 fusion.25
  357.0 0.6 pad_maximum_fusion
  357.6 0.0 all-gather.15.cloned.1.call-update
  357.6 0.0 all-reduce.2.cloned.1.call-start
  357.7 0.0 all-to-all-done
  357.7 6.7 %reshape.197 = bf16[8192,1,128]{2,1,0:T(2,128)(2,1)} reshape(bf16[16,2,32768]{2,1,0:T(2,128)(2,1)S(1)} %all-to-all-done) | data formatting | bytes 4194304
  364.5 2.5 copy.27
  366.9 2.6 copy.22
  369.6 70.9 %all-gather.15.cloned.1.call-done = bf16[2048,384]{0,1:T(8,128)(2,1)} async-done(((bf16[128,384]{0,1:T(8,128)(2,1)}), bf16[2048,384]{0,1:T(8,128)(2,1)}) %all-gather.15.cloned.1.call-update) | async-done | bytes 1572880 | tf_op jit(solution)/shard_map/all_gather | solution.py:97
  440.5 3.8 fusion.18
  444.2 0.0 all-reduce.2.cloned.1.call-update
  444.3 0.7 copy.23
  445.0 218.4 %all-reduce.2.cloned.1.call-done = bf16[512,384]{0,1:T(8,128)(2,1)} async-done(((bf16[512,384]{0,1:T(8,128)(2,1)}), bf16[512,384]{0,1:T(8,128)(2,1)}) %all-reduce.2.cloned.1.call-update) | async-done | bytes 393232 | tf_op jit(solution)/shard_map/psum | solution.py:98
  663.4 1.9 copy.24
  (4 shorter events, 0.0 us)
Async XLA Ops:
  7.2 127.3 %all-gather.9.cloned.1.call-start = ((), (), s32[]{:S(2)}) async-start(), calls=%async_computation.1 | async-start | bytes 6684672 | tf_op jit(solution)/shard_map/all_gather | solution.py:44
  7.9 133.3 %copy-start = (bf16[1,128,8192]{2,1,0:T(8,128)(2,1)S(1)}, bf16[1,128,8192]{2,1,0:T(8,128)(2,1)}, u32[]{:S(2)}) copy-start(bf16[1,128,8192]{2,1,0:T(8,128)(2,1)} %param.3) | copy-start | bytes 6291460
  7.9 199.3 %all-gather.11.cloned.1.call-start = ((), (), s32[]{:S(2)}) async-start(), calls=%async_computation.2 | async-start | bytes 2162688 | tf_op jit(solution)/shard_map/all_gather | solution.py:50
  139.9 136.2 %all-gather.13.cloned.1.call-start = ((), (), s32[]{:S(2)}) async-start(), calls=%async_computation.3 | async-start | bytes 1081344 | tf_op jit(solution)/shard_map/all_gather | solution.py:74
  140.6 207.2 %all-gather.17.cloned.1.call-start = ((), (), s32[]{:S(2)}) async-start(), calls=%async_computation.6 | async-start | bytes 1081344 | tf_op jit(solution)/shard_map/all_gather | solution.py:75
  195.9 7.6 %copy-start.3 = (bf16[1,128,128]{2,1,0:T(8,128)(2,1)S(1)}, bf16[1,128,128]{2,1,0:T(8,128)(2,1)}, u32[]{:S(2)}) copy-start(bf16[1,128,128]{2,1,0:T(8,128)(2,1)} %param.5) | copy-start | bytes 98308
  195.9 161.8 %all-to-all-start = ((bf16[16,2,32768]{2,1,0:T(2,128)(2,1)}), bf16[16,2,32768]{2,1,0:T(2,128)(2,1)S(1)}, u32[]{:S(2)}, u32[]{:S(2)}) async-start(bf16[16,2,32768]{2,1,0:T(2,128)(2,1)} %reshape.196), calls=%async_computation | async-start | bytes 4194304 | tf_op jit(solution)/shard_map/all_to_all | solution.py:40
  203.5 237.0 %all-gather.15.cloned.1.call-start = ((), (), s32[]{:S(2)}) async-start(), calls=%async_computation.4 | async-start | bytes 1671168 | tf_op jit(solution)/shard_map/all_gather | solution.py:97
  207.2 2.4 copy-start.4
  209.1 1.3 copy-start.2
  347.8 2.4 copy-start.1
  357.6 305.7 %all-reduce.2.cloned.1.call-start = ((), (), s32[]{:S(2)}) async-start(), calls=%async_computation.5 | async-start | bytes 786432 | tf_op jit(solution)/shard_map/psum | solution.py:98
Sparse Core Ops, SparseCore 0:
  11.2 123.2 all-gather.8
  140.0 67.1 all-gather.10
  209.9 66.0 all-gather.12
  278.1 69.7 all-gather.16
  357.8 82.6 all-gather.14
  444.4 218.9 all-reduce.1
where the time goes:
time: 672 us
  waiting for transfers between devices  492 us (73%)
  blocking collectives  63.1 us (9%)
  other arithmetic  46.4 us (7%)
  local copies, waits for them, and re-layouts  25.4 us (4%)
  matrix products  23.5 us (3%)
  between operations  14.2 us (2%)
  starting transfers between devices  7.83 us (1%)
    psum x1, waiting for transfers between devices, on_device(): weight_total = lax.psum(partial_sum.astype(jnp.bfloat16), 'ctx')  218 us
    all_gather x1, waiting for transfers between devices, on_device(): lax.all_gather(qkv_weight, 'dp', axis=0, tiled=True)  127 us
    all_gather x1, waiting for transfers between devices, on_device(): lax.all_gather(grad_rows, 'dp', axis=0, tiled=True)  70.9 us
    all_gather x1, waiting for transfers between devices, on_device(): lax.all_gather(cotangent, 'ctx', axis=0, tiled=True)  68.4 us
    unnamed x1, other arithmetic  45.2 us
    all_gather x1, blocking collectives, on_device(): lax.all_gather(row_delta, 'ctx', axis=0, tiled=True)  32.5 us
    all_gather x1, blocking collectives, on_device(): lax.all_gather(log_total, 'ctx', axis=0, tiled=True)  30.6 us
    unnamed x18, local copies, waits for them, and re-layouts  21.5 us
  transfers between devices with their start and end apart: 7, of which 6 were waited for; matrix products, arithmetic and copies ran while one was open for 13% of the time, Pallas kernels for 0%

commit v1 on v0

--- a/solution.py
+++ b/solution.py
@@ -6,6 +6,7 @@
 
 z_weight = 0.001
 masked_fill = -1e30
+answer_array = lambda sheet, which_axis: lax.all_gather(sheet, axis_name=which_axis).sum(axis=0)
 
 
 def stored_positions(first_row, number, half_rows, ctx_count):
@@ -95,7 +96,7 @@
     grad_value = contract_first(probs_back.astype(jnp.bfloat16), cotangent_all).astype(jnp.bfloat16)
     grad_rows = jnp.concatenate([grad_query, grad_key, grad_value], axis=1)
     partial_sum = contract_first(flat_columns, lax.all_gather(grad_rows, "dp", axis=0, tiled=True))
-    weight_total = lax.psum(partial_sum.astype(jnp.bfloat16), "ctx")
+    weight_total = answer_array(partial_sum.astype(jnp.bfloat16), "ctx")
     return (attn_rows[None], weight_total)
 
 

time: 672 us -> 559 us (0.83)
  the two profiles are of different devices: /device:TPU:4 before, /device:TPU:1 now
where the time goes in v1:
time: 559 us
  waiting for transfers between devices  359 us (64%)
  blocking collectives  62.8 us (11%)
  other arithmetic  56.6 us (10%)
  local copies, waits for them, and re-layouts  37.2 us (7%)
  matrix products  23.5 us (4%)
  between operations  14.3 us (3%)
    all_gather x1, waiting for transfers between devices, on_device(): lax.all_gather(qkv_weight, 'dp', axis=0, tiled=True)  129 us
    all_gather x1, waiting for transfers between devices, lax.all_gather(sheet, axis_name=which_axis).sum(axis=0)  83.3 us
    all_gather x1, waiting for transfers between devices, on_device(): lax.all_gather(grad_rows, 'dp', axis=0, tiled=True)  69.1 us
    all_gather x1, waiting for transfers between devices, on_device(): lax.all_gather(cotangent, 'ctx', axis=0, tiled=True)  68.5 us
    unnamed x1, other arithmetic  45.2 us
    unnamed x19, local copies, waits for them, and re-layouts  33.3 us
    all_gather x1, blocking collectives, on_device(): lax.all_gather(row_delta, 'ctx', axis=0, tiled=True)  32.2 us
    all_gather x1, blocking collectives, on_device(): lax.all_gather(log_total, 'ctx', axis=0, tiled=True)  30.6 us
  transfers between devices with their start and end apart: 7, of which 6 were waited for; matrix products, arithmetic and copies ran while one was open for 15% of the time, Pallas kernels for 0%

profile of v1, /device:TPU:1, one launch (start us, length us, event | category | flops | bytes accessed | tf_op | source)
XLA Modules:
  0.0 558.8 jit_solution(15063627960101908648)
XLA Ops:
  7.2 0.0 all-gather.11.cloned.1.call-start
  7.2 0.7 all-gather.11.cloned.1.call-update
  7.9 0.0 copy-start
  7.9 0.0 all-gather.13.cloned.1.call-start
  8.0 128.5 %all-gather.11.cloned.1.call-done = bf16[8192,384]{1,0:T(8,128)(2,1)} async-done(((bf16[512,384]{1,0:T(8,128)(2,1)}), bf16[8192,384]{1,0:T(8,128)(2,1)}) %all-gather.11.cloned.1.call-update) | async-done | bytes 6291472 | tf_op jit(solution)/shard_map/all_gather | solution.py:45
  136.5 4.7 fusion.19
  141.2 0.6 slice.27
  141.8 0.0 all-gather.13.cloned.1.call-update
  141.8 0.0 all-gather.15.cloned.1.call-start
  141.9 0.6 slice.26
  142.5 0.1 all-gather.15.cloned.1.call-update
  142.6 0.0 all-gather.19.cloned.1.call-start
  142.6 0.5 all-gather.19.cloned.1.call-update
  143.2 0.0 copy-done
  143.2 6.8 %copy.18 = bf16[1,128,8192]{1,0,2:T(2,128)(2,1)} copy(bf16[1,128,8192]{2,1,0:T(8,128)(2,1)S(1)} %copy-done) | data formatting | bytes 4194304 | tf_op args[0]
  150.0 0.6 broadcast.369
  150.6 45.2 %reduce.1 = bf16[8192,128]{1,0:T(8,128)(2,1)S(1)} reduce(bf16[8192,1,128]{2,1,0:T(2,128)(2,1)} %bitcast.64, bf16[]{:T(256)} %broadcast.369), dimensions={1}, to_apply=%bitcast.57.reduce_sub_computation | reduce | bytes 4194306
  195.8 2.1 reshape.197
  197.8 0.0 copy-start.3
  197.8 4.8 all-to-all-start
  202.7 0.0 all-gather.17.cloned.1.call-start
  202.7 0.0 copy-done.3
  202.8 0.1 copy.15
  202.9 5.9 %all-gather.13.cloned.1.call-done = bf16[4096,256]{1,0:T(8,128)(2,1)} async-done(((bf16[128,256]{1,0:T(8,128)(2,1)}), bf16[4096,256]{1,0:T(8,128)(2,1)}) %all-gather.13.cloned.1.call-update) | async-done | bytes 2097168 | tf_op jit(solution)/shard_map/all_gather | solution.py:51
  208.8 0.0 copy-start.4
  208.8 1.9 fusion.69
  210.7 0.0 copy-start.2
  210.7 0.4 exponential_reduce_fusion
  211.1 0.0 copy-done.4
  211.2 0.7 multiply_reduce_fusion
  211.9 0.1 copy-done.2
  212.0 32.2 %all-gather.3 = f32[32,1,128]{2,1,0:T(1,128)S(1)} all-gather(f32[1,1,128]{2,1,0:T(1,128)S(1)} %bitcast.74), channel_id=1, replica_groups=mesh['dp'=16,'ctx'=32] {'ctx'}, dimensions={0}, use_global_device_ids=true | all-gather | bytes 16896 | tf_op jit(solution)/shard_map/all_gather | solution.py:80
  244.2 30.6 %all-gather.2 = f32[32,1,128]{2,1,0:T(1,128)S(1)} all-gather(f32[1,1,128]{2,1,0:T(1,128)S(1)} %bitcast.73), channel_id=1, replica_groups=mesh['dp'=16,'ctx'=32] {'ctx'}, dimensions={0}, use_global_device_ids=true | all-gather | bytes 16896 | tf_op jit(solution)/shard_map/all_gather | solution.py:79
  274.8 2.8 all-gather.15.cloned.1.call-done
  277.6 3.3 fusion.6
  280.9 68.5 %all-gather.19.cloned.1.call-done = bf16[1,4096,128]{2,1,0:T(8,128)(2,1)} async-done(((bf16[1,128,128]{2,1,0:T(8,128)(2,1)}), bf16[1,4096,128]{2,1,0:T(8,128)(2,1)}) %all-gather.19.cloned.1.call-update) | async-done | bytes 1048592 | tf_op jit(solution)/shard_map/all_gather | solution.py:76
  349.4 0.0 copy-start.1
  349.4 2.4 convolution_convert_fusion.1
  351.8 0.0 copy-done.1
  351.8 3.5 fusion.24
  355.4 3.2 fusion.25
  358.5 0.6 pad_maximum_fusion
  359.2 0.0 all-gather.17.cloned.1.call-update
  359.2 0.0 all-gather.21.cloned.1.call-start
  359.3 0.0 all-to-all-done
  359.3 6.7 %reshape.198 = bf16[8192,1,128]{2,1,0:T(2,128)(2,1)} reshape(bf16[16,2,32768]{2,1,0:T(2,128)(2,1)S(1)} %all-to-all-done) | data formatting | bytes 4194304
  366.0 2.5 copy.24
  368.5 2.6 copy.19
  371.1 69.1 %all-gather.17.cloned.1.call-done = bf16[2048,384]{0,1:T(8,128)(2,1)} async-done(((bf16[128,384]{0,1:T(8,128)(2,1)}), bf16[2048,384]{0,1:T(8,128)(2,1)}) %all-gather.17.cloned.1.call-update) | async-done | bytes 1572880 | tf_op jit(solution)/shard_map/all_gather | solution.py:98
  440.2 3.8 fusion.18
  444.0 0.0 all-gather.21.cloned.1.call-update
  444.0 0.7 copy.20
  444.7 83.3 %all-gather.21.cloned.1.call-done = bf16[16384,384]{0,1:T(8,128)(2,1)} async-done(((bf16[512,384]{0,1:T(8,128)(2,1)}), bf16[16384,384]{0,1:T(8,128)(2,1)}) %all-gather.21.cloned.1.call-update) | async-done | bytes 12582928 | tf_op jit(solution)/shard_map/all_gather | solution.py:9
  528.0 12.8 %copy.25 = bf16[48,8,32,512]{3,2,1,0:T(8,128)(2,1)} copy(bf16[48,8,32,512]{3,1,2,0:T(8,128)(2,1)} %bitcast.66) | data formatting | bytes 25165824
  540.8 10.2 %bitcast_reduce_fusion = bf16[512,384]{0,1:T(8,128)(2,1)S(1)} fusion(bf16[48,8,32,512]{3,2,1,0:T(8,128)(2,1)} %copy.25), kind=kLoop, calls=%fused_computation | loop fusion | flops 6094848 | bytes 12976128 | tf_op jit(solution)/shard_map/reduce_sum | solution.py:9
  551.1 0.9 copy.21
  (4 shorter events, 0.0 us)
Async XLA Ops:
  7.2 129.3 %all-gather.11.cloned.1.call-start = ((), (), s32[]{:S(2)}) async-start(), calls=%async_computation.1 | async-start | bytes 6684672 | tf_op jit(solution)/shard_map/all_gather | solution.py:45
  7.9 135.3 %copy-start = (bf16[1,128,8192]{2,1,0:T(8,128)(2,1)S(1)}, bf16[1,128,8192]{2,1,0:T(8,128)(2,1)}, u32[]{:S(2)}) copy-start(bf16[1,128,8192]{2,1,0:T(8,128)(2,1)} %param.3) | copy-start | bytes 6291460
  7.9 200.9 %all-gather.13.cloned.1.call-start = ((), (), s32[]{:S(2)}) async-start(), calls=%async_computation.2 | async-start | bytes 2162688 | tf_op jit(solution)/shard_map/all_gather | solution.py:51
  141.8 135.8 %all-gather.15.cloned.1.call-start = ((), (), s32[]{:S(2)}) async-start(), calls=%async_computation.3 | async-start | bytes 1081344 | tf_op jit(solution)/shard_map/all_gather | solution.py:75
  142.6 206.8 %all-gather.19.cloned.1.call-start = ((), (), s32[]{:S(2)}) async-start(), calls=%async_computation.5 | async-start | bytes 1081344 | tf_op jit(solution)/shard_map/all_gather | solution.py:76
  197.8 4.9 copy-start.3
  197.8 161.4 %all-to-all-start = ((bf16[16,2,32768]{2,1,0:T(2,128)(2,1)}), bf16[16,2,32768]{2,1,0:T(2,128)(2,1)S(1)}, u32[]{:S(2)}, u32[]{:S(2)}) async-start(bf16[16,2,32768]{2,1,0:T(2,128)(2,1)} %reshape.197), calls=%async_computation | async-start | bytes 4194304 | tf_op jit(solution)/shard_map/all_to_all | solution.py:41
  202.7 237.5 %all-gather.17.cloned.1.call-start = ((), (), s32[]{:S(2)}) async-start(), calls=%async_computation.4 | async-start | bytes 1671168 | tf_op jit(solution)/shard_map/all_gather | solution.py:98
  208.8 2.4 copy-start.4
  210.7 1.3 copy-start.2
  349.4 2.4 copy-start.1
  359.2 168.8 %all-gather.21.cloned.1.call-start = ((), (), s32[]{:S(2)}) async-start(), calls=%async_computation.6 | async-start | bytes 12976128 | tf_op jit(solution)/shard_map/all_gather | solution.py:9
Sparse Core Ops, SparseCore 0:
  11.2 125.2 all-gather.10
  142.0 66.7 all-gather.12
  211.5 66.0 all-gather.14
  279.6 69.7 all-gather.18
  359.3 80.8 all-gather.16
  444.1 83.8 all-gather.20
